TPU v7x, 32 devices: a whole 2x2x4 slice. The times are simulated.
32 devices in a mesh: space: 8 (over y, x, core), mode: 4 (over z).
Axes of the slice: x: 2, y: 2, z: 4, core: 2. Of those that a mesh axis runs over, the one named last changes fastest.
Arguments:
- start_modes: float32 [256, 24576], P('mode', 'space')
- hessian: bfloat16 [128, 8, 192, 192], P('space'), may hold values from -0.15625 to 0.15625
- block_exponent: int32 [128, 8], P('space'), may hold values from -1 to 1
- col_block: int32 [128, 8], P('space'), may hold values from 0 to 19, as said below
- grain_count: int32 [8], P('space'), may hold values from 384 to 512, as said below
Outputs:
- modes: float32 [256, 24576], P('mode', 'space')
Inputs may be any that keep to these rules, and one draw needn't show every extreme that they name: col_block[b, k] lies between b mod 16 and b mod 16 + 2 * 2; slot 0 is b mod 16 + 2; both ends are reached in every slab. `grain_count`: at most 512 grains a slab, reached by at least one slab.
All inputs are finite; a program needn't handle non-finite values.
Results may differ from a plain program's by a relative error of at most 0.0034.
Values may be sent and summed in bfloat16 or wider, within the bound.
A program may use at most 64 MiB of HBM per device.

v0:
```python
import jax
import jax.numpy as jnp
from jax import lax
from jax.sharding import PartitionSpec as P

HALO_BLOCKS = 2
filter_center = -0.5
filter_half = 1.5


def extended(cells, sides, width):
    for axis, dim in sides:
        count = lax.axis_size(axis)
        head = lax.slice_in_dim(cells, 0, width, axis=dim)
        tail = lax.slice_in_dim(cells, cells.shape[dim] - width, cells.shape[dim], axis=dim)
        cells = jnp.concatenate(
            [
                lax.ppermute(tail, axis, [(i, (i + 1) % count) for i in range(count)]),
                cells,
                lax.ppermute(head, axis, [((i + 1) % count, i) for i in range(count)]),
            ],
            axis=dim,
        )
    return cells


def per_device(start_modes, hessian, block_exponent, col_block, grain_count):
    panel_size, rows_here = start_modes.shape
    slab_blocks, contacts, block_size, _ = hessian.shape
    halo_width = HALO_BLOCKS * block_size
    places = lax.broadcasted_iota(jnp.int32, (rows_here,), 0)
    live = (places < 6 * grain_count[0]).astype(jnp.float32)
    scales = jnp.exp2(block_exponent.astype(jnp.float32)).astype(jnp.bfloat16)

    def operate(vectors_low):
        padded = extended(vectors_low, (("space", 1),), halo_width)
        window = padded.reshape(panel_size, slab_blocks + 2 * HALO_BLOCKS, block_size)
        gathered = jnp.take(window, col_block, axis=1)
        gathered = gathered * scales[None, :, :, None]
        image = jnp.einsum("rkij,prkj->pri", hessian, gathered, preferred_element_type=jnp.float32)
        return image.reshape(panel_size, rows_here)

    start = start_modes * live
    image = operate(start.astype(jnp.bfloat16))
    first = (image - filter_center * start) / filter_half * live
    image = operate(first.astype(jnp.bfloat16))
    second = (2.0 * (image - filter_center * first) / filter_half - start) * live
    my_index = lax.axis_index("mode")
    whole = lax.all_gather(second, "mode", axis=0, tiled=True)
    partial_rows = jnp.dot(
        second, whole.T, precision=lax.Precision.HIGHEST, preferred_element_type=jnp.float32
    )
    summed_rows = lax.psum(partial_rows, "space")
    gram = lax.all_gather(summed_rows, "mode", axis=0, tiled=True)
    lower_factor = jnp.linalg.cholesky(gram)
    identity_matrix = jnp.eye(gram.shape[0], dtype=jnp.float32)
    inverse_factor = jax.scipy.linalg.solve_triangular(lower_factor, identity_matrix, lower=True)
    own_inverse = lax.dynamic_slice_in_dim(inverse_factor, my_index * panel_size, panel_size, 0)
    return jnp.dot(
        own_inverse, whole, precision=lax.Precision.HIGHEST, preferred_element_type=jnp.float32
    )


def solution(mesh):
    return jax.shard_map(
        per_device,
        mesh=mesh,
        in_specs=(
            P("mode", "space"),
            P("space", None, None, None),
            P("space", None),
            P("space", None),
            P("space"),
        ),
        out_specs=P("mode", "space"),
        check_vma=False,
    )
```

profile of v0, /device:TPU:0, one launch (start us, length us, event | category | flops | bytes accessed | tf_op | source)
XLA Modules:
  0.0 278.4 jit_solution(5893356217424159986)
XLA Ops:
  6.5 0.0 all-gather.2.cloned.1.call-start
  7.2 1.2 multiply_convert_fusion
  8.4 0.5 collective-permute-start
  9.0 2.9 %collective-permute-start.1 = (bf16[64,384]{1,0:T(8,128)(2,1)S(1)}, bf16[64,384]{1,0:T(8,128)(2,1)S(1)}, u32[]{:S(2)}, u32[]{:S(2)}) collective-permute-start(bf16[64,384]{1,0:T(8,128)(2,1)S(1)} %get-tuple-element.27), channel_id=1, source_target_pairs={{4,0},{8,4},{12,8},{16,12},{20,16},{24,20},{28,24},{0,28},{5,1},{9... | collective-permute-start | bytes 147464 | tf_op jit(solution)/shard_map/ppermute | solution.py:20
  11.9 0.7 compare_select_fusion
  12.6 0.7 compare_and_fusion
  13.3 0.1 copy.28
  13.4 0.1 reshape.87
  13.4 0.7 exponential_convert_fusion
  14.1 0.1 copy.30
  14.2 0.1 copy.26
  14.3 0.0 collective-permute-done
  14.3 0.0 collective-permute-done.1
  14.4 0.8 reshape.44
  15.2 0.1 copy.29
  15.3 2.8 gather_fusion
  18.1 11.0 %fusion.10 = f32[64,16,192]{2,0,1:T(8,128)} fusion(bf16[16,8,192,192]{3,2,1,0:T(8,128)(2,1)} %param.8, bf16[16,8,64,192]{3,2,1,0:T(8,128)(2,1)} %bitcast.60, pred[16,8]{1,0:T(8,128)(4,1)S(1)} %copy.26, bf16[16,8]{1,0:T(8,128)(2,1)S(1)} %copy.30), kind=kOutput, calls=%fused_computation.16 | convolution fusion | flops 607125504 | bytes 13369728 | tf_op jit(solution)/shard_map/rkij,prkj->pri/dot_general | solution.py:40
  29.1 1.9 copy.31
  31.0 0.4 reshape.45
  31.4 0.0 copy-done.1
  31.4 0.1 fusion.12
  31.5 0.8 collective-permute-start.2
  32.3 1.9 collective-permute-start.3
  34.2 1.8 collective-permute-done.2
  36.0 0.0 collective-permute-done.3
  36.0 0.8 pad_maximum_fusion.1
  36.8 1.9 reshape.46
  38.7 0.1 copy.33
  38.9 2.8 gather_fusion.1
  41.6 11.0 %fusion.11 = f32[64,16,192]{2,0,1:T(8,128)} fusion(bf16[16,8,192,192]{3,2,1,0:T(8,128)(2,1)} %param.8, bf16[16,8,64,192]{3,2,1,0:T(8,128)(2,1)} %bitcast.59, pred[16,8]{1,0:T(8,128)(4,1)S(1)} %copy.26, bf16[16,8]{1,0:T(8,128)(2,1)S(1)} %copy.30), kind=kOutput, calls=%fused_computation.17 | convolution fusion | flops 607125504 | bytes 13369728 | tf_op jit(solution)/shard_map/rkij,prkj->pri/dot_general | solution.py:40
  52.6 1.8 copy.34
  54.4 1.3 reshape.47
  55.7 2.3 subtract_multiply_fusion
  58.0 0.0 all-gather.2.cloned.1.call-update
  58.0 0.2 all-reduce.3.cloned.1.call-start
  58.2 65.6 %all-gather.2.cloned.1.call-done = f32[256,3072]{1,0:T(8,128)} async-done(((f32[64,3072]{1,0:T(8,128)}), f32[256,3072]{1,0:T(8,128)}) %all-gather.2.cloned.1.call-update) | async-done | bytes 3145744 | tf_op jit(solution)/shard_map/all_gather | solution.py:49
  123.8 5.9 %fusion.33 = f32[64,256]{1,0:T(8,128)} fusion(f32[64,3072]{1,0:T(8,128)} %subtract_multiply_fusion, f32[256,3072]{1,0:T(8,128)} %all-gather.2.cloned.1.call-done), kind=kOutput, calls=%fused_computation.68 | convolution fusion | flops 603979776 | bytes 3997696 | tf_op jit(solution)/shard_map/dot_general | solution.py:50
  129.7 0.0 all-reduce.3.cloned.1.call-update
  129.7 52.0 %all-reduce.3.cloned.1.call-done = f32[64,256]{1,0:T(8,128)} async-done(((f32[64,256]{1,0:T(8,128)}), f32[64,256]{1,0:T(8,128)}) %all-reduce.3.cloned.1.call-update) | async-done | bytes 65552 | tf_op jit(solution)/shard_map/psum | solution.py:53
  181.7 14.1 %all_gather.7 = f32[256,256]{1,0:T(8,128)S(1)} all-gather(f32[64,256]{1,0:T(8,128)} %all-reduce.3.cloned.1.call-done), channel_id=1, replica_groups=mesh['space'=8,'mode'=4] {'mode'}, dimensions={0}, use_global_device_ids=true | all-gather | bytes 327680 | tf_op jit(solution)/shard_map/all_gather | solution.py:54
  195.9 0.8 copy.35
  196.7 1.0 fusion.13
  197.7 0.0 copy-start.3
  197.7 0.7 copy-done.3
  198.4 11.7 %cholesky.50 = f32[128,128]{1,0:T(8,128)S(1)} custom-call(f32[128,128]{1,0:T(8,128)S(1)} %cholesky.118), custom_call_target="Cholesky" | custom-call | tf_op jit(solution)/shard_map/jit(cholesky)/cholesky | solution.py:55
  210.1 0.6 select_reduce_fusion.1
  210.8 10.6 %custom-call.15 = f32[1,128,128]{1,2,0:T(8,128)S(1)} custom-call(f32[1,128,128]{2,1,0:T(8,128)} %get-tuple-element.31), custom_call_target="InvertDiagBlocksLowerTriangular" | custom-call | tf_op jit(solution)/shard_map/jit(cholesky)/cholesky | solution.py:55
  221.4 1.0 constant_dynamic-update-slice_fusion
  222.5 1.7 convolution_subtract_fusion.1
  224.2 12.5 %cholesky.105 = f32[128,128]{1,0:T(8,128)S(1)} custom-call(f32[128,128]{1,0:T(8,128)} %convolution_subtract_fusion.1), custom_call_target="Cholesky" | custom-call | tf_op jit(solution)/shard_map/jit(cholesky)/cholesky | solution.py:55
  236.8 0.7 compare_reduce_fusion
  238.8 1.0 select_select_fusion
  239.8 0.1 triangular_solve.63
  239.8 5.2 %while.1 = (s32[]{:T(128)}, f32[256,256]{1,0:T(8,128)S(1)}, s32[2,2]{1,0:T(2,128)S(1)}, f32[2,128,128]{2,1,0:T(8,128)}, s32[]{:T(128)}) while((s32[]{:T(128)}, f32[256,256]{1,0:T(8,128)S(1)}, s32[2,2]{1,0:T(2,128)S(1)}, f32[2,128,128]{2,1,0:T(8,128)}, s32[]{:T(128)}) %tuple.26), condition=%wide.while_cond, body=%wide.while_body.sunk | while | flops 2 | bytes 132705 | solution.py:57
  240.0 0.6 fusion.44
  240.6 1.9 bitcast_dynamic-update-slice_fusion.2
  242.5 0.6 fusion.44
  243.1 1.9 bitcast_dynamic-update-slice_fusion.2
  245.0 21.1 %custom-call.16 = f32[2,128,128]{1,2,0:T(8,128)} custom-call(f32[2,128,128]{2,1,0:T(8,128)} %get-tuple-element.13), custom_call_target="InvertDiagBlocksLowerTriangular" | custom-call | tf_op jit(solution)/shard_map/jit(_solve_triangular)/triangular_solve | solution.py:57
  266.1 1.1 fusion.14
  267.2 0.3 convolution_subtract_fusion
  267.5 1.2 fusion.20
  268.7 0.0 copy-done
  268.7 2.9 %fusion.17 = f32[64,3072]{1,0:T(8,128)} fusion(f32[256,3072]{1,0:T(8,128)S(1)} %copy-done, s32[]{:T(128)S(6)} %select_n.15, f32[128,256]{1,0:T(8,128)S(1)} %fusion.14, f32[128,256]{1,0:T(8,128)S(1)} %fusion.20), kind=kOutput, calls=%fused_computation.36 | convolution fusion | flops 603996160 | bytes 4194308 | tf_op jit(solution)/shard_map/dot_general | solution.py:59
  (18 shorter events, 0.2 us)
Async XLA Ops:
  6.5 117.3 %all-gather.2.cloned.1.call-start = ((), (), s32[]{:S(2)}) async-start(), calls=%async_computation | async-start | bytes 3932160 | tf_op jit(solution)/shard_map/all_gather | solution.py:49
  8.4 5.9 %collective-permute-start = (bf16[64,384]{1,0:T(8,128)(2,1)S(1)}, bf16[64,384]{1,0:T(8,128)(2,1)S(1)}, u32[]{:S(2)}, u32[]{:S(2)}) collective-permute-start(bf16[64,384]{1,0:T(8,128)(2,1)S(1)} %get-tuple-element.26), channel_id=1, source_target_pairs={{0,4},{4,8},{8,12},{12,16},{16,20},{20,24},{24,28},{28,0},{1,5},{5... | collective-permute-start | bytes 147464 | tf_op jit(solution)/shard_map/ppermute | solution.py:18
  9.0 5.4 %collective-permute-start.1 = (bf16[64,384]{1,0:T(8,128)(2,1)S(1)}, bf16[64,384]{1,0:T(8,128)(2,1)S(1)}, u32[]{:S(2)}, u32[]{:S(2)}) collective-permute-start(bf16[64,384]{1,0:T(8,128)(2,1)S(1)} %get-tuple-element.27), channel_id=1, source_target_pairs={{4,0},{8,4},{12,8},{16,12},{20,16},{24,20},{28,24},{0,28},{5,1},{9... | collective-permute-start | bytes 147464 | tf_op jit(solution)/shard_map/ppermute | solution.py:20
  29.1 2.3 copy-start.1
  31.5 4.5 %collective-permute-start.2 = (bf16[64,384]{1,0:T(8,128)(2,1)S(1)}, bf16[64,384]{1,0:T(8,128)(2,1)S(1)}, u32[]{:S(2)}, u32[]{:S(2)}) collective-permute-start(bf16[64,384]{1,0:T(8,128)(2,1)S(1)} %get-tuple-element.24), channel_id=1, source_target_pairs={{0,4},{4,8},{8,12},{12,16},{16,20},{20,24},{24,28},{28,0},{1,5},{5... | collective-permute-start | bytes 147464 | tf_op jit(solution)/shard_map/ppermute | solution.py:18
  32.3 3.7 %collective-permute-start.3 = (bf16[64,384]{1,0:T(8,128)(2,1)S(1)}, bf16[64,384]{1,0:T(8,128)(2,1)S(1)}, u32[]{:S(2)}, u32[]{:S(2)}) collective-permute-start(bf16[64,384]{1,0:T(8,128)(2,1)S(1)} %get-tuple-element.25), channel_id=1, source_target_pairs={{4,0},{8,4},{12,8},{16,12},{20,16},{24,20},{28,24},{0,28},{5,1},{9... | collective-permute-start | bytes 147464 | tf_op jit(solution)/shard_map/ppermute | solution.py:20
  58.0 123.8 %all-reduce.3.cloned.1.call-start = ((), (), s32[]{:S(2)}) async-start(), calls=%async_computation.1 | async-start | bytes 131072 | tf_op jit(solution)/shard_map/psum | solution.py:53
  123.8 144.9 %copy-start = (f32[256,3072]{1,0:T(8,128)S(1)}, f32[256,3072]{1,0:T(8,128)}, u32[]{:S(2)}) copy-start(f32[256,3072]{1,0:T(8,128)} %all-gather.2.cloned.1.call-done) | copy-start | bytes 9437188
  197.7 0.7 copy-start.3
  236.8 2.0 copy-start.2
Sparse Core Ops, SparseCore 0:
  58.1 65.6 all-gather.1
  129.8 51.8 all-reduce.2
where the time goes:
time: 279 us; the launch traced here: 278 us
  waiting for transfers between devices  119 us (43%)
  other arithmetic  65.9 us (24%)
  matrix products  36 us (13%)
  local copies, waits for them, and re-layouts  20.9 us (7%)
  between operations  15.5 us (6%)
  blocking collectives  14.1 us (5%)
  starting transfers between devices  6.4 us (2%)
    all_gather x1, waiting for transfers between devices, per_device(): whole = lax.all_gather(second, 'mode', axis=0, tiled=True)  65.6 us
    psum x1, waiting for transfers between devices, per_device(): summed_rows = lax.psum(partial_rows, 'space')  52 us
    another operation x6, other arithmetic, per_device(): lower_factor = jnp.linalg.cholesky(gram)  36.3 us
    another operation x3, other arithmetic, per_device(): jax.scipy.linalg.solve_triangular(lower_factor, identity_matrix, lower=True)  22.1 us
    dot_general x2, matrix products, operate(): jnp.einsum('rkij,prkj->pri', hessian, gathered, preferred_element_type=jn...  22 us
    all_gather x1, blocking collectives, per_device(): gram = lax.all_gather(summed_rows, 'mode', axis=0, tiled=True)  14.1 us
    dot_general x1, matrix products, per_device(): jnp.dot(second, whole.T, precision=lax.Precision.HIGHEST, preferred_eleme...  5.88 us
  transfers between devices with their start and end apart: 6, of which 3 were waited for; matrix products, arithmetic and copies ran while one was open for 1% of the time, Pallas kernels for 0%

commit v1 on v0

--- a/solution.py
+++ b/solution.py
@@ -46,7 +46,12 @@
     image = operate(first.astype(jnp.bfloat16))
     second = (2.0 * (image - filter_center * first) / filter_half - start) * live
     my_index = lax.axis_index("mode")
-    whole = lax.all_gather(second, "mode", axis=0, tiled=True)
+    ring = [second]
+    for hop in range(3):
+        ring.append(lax.ppermute(ring[-1], "mode", [(dev, (dev + 1) % 4) for dev in range(4)]))
+    whole = jnp.roll(
+        jnp.concatenate(ring[::-1], axis=0), (lax.axis_index("mode") + 1) * ring[0].shape[0], axis=0
+    )
     partial_rows = jnp.dot(
         second, whole.T, precision=lax.Precision.HIGHEST, preferred_element_type=jnp.float32
     )

time: 279 us -> 263 us (0.943)
  other arithmetic: 65.9 us -> 58.6 us
  waiting for transfers between devices: 119 us -> 114 us
  matrix products: 36 us -> 31.7 us
    all_gather x1 -> x0, waiting for transfers between devices: 65.6 us -> none  [per_device(): whole = lax.all_gather(second, 'mode', axis=0, tiled=True)]
    ppermute x0 -> x3, waiting for transfers between devices: none -> 61.4 us  [per_device(): lax.ppermute(ring[-1], 'mode', [(dev, (dev + 1) % 4) for dev in range(4)])]
  transfers between devices with their start and end apart: 6 -> 8, of which waited for: 3 -> 5; matrix products, arithmetic and copies ran while one was open for 1% -> 1% of each run, Pallas kernels for 0% -> 0%
where the time goes in v1:
time: 263 us
  waiting for transfers between devices  114 us (43%)
  other arithmetic  58.6 us (22%)
  matrix products  31.7 us (12%)
  local copies, waits for them, and re-layouts  20.2 us (8%)
  between operations  15.6 us (6%)
  blocking collectives  14.1 us (5%)
  starting transfers between devices  8.51 us (3%)
    ppermute x3, waiting for transfers between devices, per_device(): lax.ppermute(ring[-1], 'mode', [(dev, (dev + 1) % 4) for dev in range(4)])  61.4 us
    psum x1, waiting for transfers between devices, per_device(): summed_rows = lax.psum(partial_rows, 'space')  50.7 us
    another operation x6, other arithmetic, per_device(): lower_factor = jnp.linalg.cholesky(gram)  34 us
    dot_general x2, matrix products, operate(): jnp.einsum('rkij,prkj->pri', hessian, gathered, preferred_element_type=jn...  22 us
    another operation x3, other arithmetic, per_device(): jax.scipy.linalg.solve_triangular(lower_factor, identity_matrix, lower=True)  19.7 us
    all_gather x1, blocking collectives, per_device(): gram = lax.all_gather(summed_rows, 'mode', axis=0, tiled=True)  14.1 us
    gather x2, local copies, waits for them, and re-layouts, operate(): gathered = jnp.take(window, col_block, axis=1)  5.49 us
  transfers between devices with their start and end apart: 8, of which 5 were waited for; matrix products, arithmetic and copies ran while one was open for 1% of the time, Pallas kernels for 0%

profile of v1, /device:TPU:0, one launch (start us, length us, event | category | flops | bytes accessed | tf_op | source)
XLA Modules:
  0.0 263.0 jit_solution(2030854101296056298)
XLA Ops:
  7.2 1.2 multiply_convert_fusion
  8.4 0.5 collective-permute-start
  9.0 2.9 %collective-permute-start.1 = (bf16[64,384]{1,0:T(8,128)(2,1)S(1)}, bf16[64,384]{1,0:T(8,128)(2,1)S(1)}, u32[]{:S(2)}, u32[]{:S(2)}) collective-permute-start(bf16[64,384]{1,0:T(8,128)(2,1)S(1)} %get-tuple-element.27), channel_id=1, source_target_pairs={{4,0},{8,4},{12,8},{16,12},{20,16},{24,20},{28,24},{0,28},{5,1},{9... | collective-permute-start | bytes 147464 | tf_op jit(solution)/shard_map/ppermute | solution.py:20
  11.9 0.7 compare_select_fusion
  12.6 0.7 compare_and_fusion
  13.3 0.1 copy.28
  13.4 0.1 reshape.87
  13.4 0.7 exponential_convert_fusion
  14.1 0.1 copy.30
  14.2 0.1 copy.26
  14.4 0.8 reshape.44
  15.2 0.1 copy.29
  15.3 2.7 %gather_fusion = bf16[128,64,192]{2,1,0:T(8,128)(2,1)} fusion(bf16[64,20,192]{2,0,1:T(8,128)(2,1)S(1)} %copy.29, s32[1024]{0:T(1024)S(1)} %pad_clamp_fusion), kind=kCustom, calls=%fused_computation.clone | custom fusion | bytes 6291968 | tf_op jit(solution)/shard_map/jit(_take)/gather | solution.py:38
  18.1 11.0 %fusion.14 = f32[64,16,192]{2,0,1:T(8,128)} fusion(bf16[16,8,192,192]{3,2,1,0:T(8,128)(2,1)} %param.8, bf16[16,8,64,192]{3,2,1,0:T(8,128)(2,1)} %bitcast.58, pred[16,8]{1,0:T(8,128)(4,1)S(1)} %copy.26, bf16[16,8]{1,0:T(8,128)(2,1)S(1)} %copy.30), kind=kOutput, calls=%fused_computation.20 | convolution fusion | flops 607125504 | bytes 13369728 | tf_op jit(solution)/shard_map/rkij,prkj->pri/dot_general | solution.py:40
  29.1 1.8 copy.31
  30.9 0.4 reshape.45
  31.4 0.1 fusion.16
  31.5 0.8 collective-permute-start.2
  32.3 1.9 collective-permute-start.3
  34.2 1.8 collective-permute-done.2
  36.0 0.8 reshape.46
  36.8 0.1 copy.33
  37.0 2.7 %gather_fusion.1 = bf16[128,64,192]{2,1,0:T(8,128)(2,1)} fusion(bf16[64,20,192]{2,0,1:T(8,128)(2,1)S(1)} %copy.33, s32[1024]{0:T(1024)S(1)} %pad_clamp_fusion), kind=kCustom, calls=%fused_computation.1.clone | custom fusion | bytes 6291968 | tf_op jit(solution)/shard_map/jit(_take)/gather | solution.py:38
  39.7 11.0 %fusion.15 = f32[64,16,192]{2,0,1:T(8,128)} fusion(bf16[16,8,192,192]{3,2,1,0:T(8,128)(2,1)} %param.8, bf16[16,8,64,192]{3,2,1,0:T(8,128)(2,1)} %bitcast.57, pred[16,8]{1,0:T(8,128)(4,1)S(1)} %copy.26, bf16[16,8]{1,0:T(8,128)(2,1)S(1)} %copy.30), kind=kOutput, calls=%fused_computation.21 | convolution fusion | flops 607125504 | bytes 13369728 | tf_op jit(solution)/shard_map/rkij,prkj->pri/dot_general | solution.py:40
  50.7 1.8 copy.34
  52.5 1.3 reshape.47
  53.8 1.4 subtract_multiply_fusion
  55.2 2.3 collective-permute-start.4
  57.5 20.1 %collective-permute-done.4 = f32[64,3072]{1,0:T(8,128)S(1)} collective-permute-done((f32[64,3072]{1,0:T(8,128)S(1)}, f32[64,3072]{1,0:T(8,128)S(1)}, u32[]{:S(2)}, u32[]{:S(2)}) %collective-permute-start.4) | collective-permute-done | bytes 786464 | tf_op jit(solution)/shard_map/ppermute | solution.py:51
  77.6 0.0 collective-permute-start.5
  77.6 21.1 %collective-permute-done.5 = f32[64,3072]{1,0:T(8,128)S(1)} collective-permute-done((f32[64,3072]{1,0:T(8,128)S(1)}, f32[64,3072]{1,0:T(8,128)S(1)}, u32[]{:S(2)}, u32[]{:S(2)}) %collective-permute-start.5) | collective-permute-done | bytes 786464 | tf_op jit(solution)/shard_map/ppermute | solution.py:51
  98.7 0.0 collective-permute-start.6
  98.7 20.2 %collective-permute-done.6 = f32[64,3072]{1,0:T(8,128)S(1)} collective-permute-done((f32[64,3072]{1,0:T(8,128)S(1)}, f32[64,3072]{1,0:T(8,128)S(1)}, u32[]{:S(2)}, u32[]{:S(2)}) %collective-permute-start.6) | collective-permute-done | bytes 786464 | tf_op jit(solution)/shard_map/ppermute | solution.py:51
  118.9 0.1 constant_dynamic-update-slice_fusion.7
  119.0 0.1 constant_dynamic-update-slice_fusion.6
  119.0 0.1 constant_dynamic-update-slice_fusion.5
  119.1 0.1 constant_dynamic-update-slice_fusion.4
  119.2 0.1 constant_dynamic-update-slice_fusion.3
  119.2 0.1 constant_dynamic-update-slice_fusion.2
  119.3 0.1 constant_dynamic-update-slice_fusion.1
  119.4 0.1 constant_dynamic-update-slice_fusion
  119.4 2.6 %copy-done = f32[512,3072]{1,0:T(8,128)} copy-done((f32[512,3072]{1,0:T(8,128)}, f32[512,3072]{1,0:T(8,128)S(1)}, u32[]{:S(2)}) %copy-start) | copy-done | bytes 6291480
  122.1 3.6 %fusion.8 = f32[64,256]{1,0:T(8,128)} fusion(f32[64,3072]{1,0:T(8,128)S(1)} %subtract_multiply_fusion, f32[512,3072]{1,0:T(8,128)S(1)} %constant_dynamic-update-slice_fusion, s32[]{:T(128)S(6)} %select_n.28), kind=kOutput, calls=%fused_computation.14 | convolution fusion | flops 603979776 | bytes 3997700 | tf_op jit(solution)/shard_map/dot_general | solution.py:55
  125.7 0.0 all-reduce.3.cloned.1.call-update
  125.7 50.7 %all-reduce.3.cloned.1.call-done = f32[64,256]{1,0:T(8,128)} async-done(((f32[64,256]{1,0:T(8,128)}), f32[64,256]{1,0:T(8,128)}) %all-reduce.3.cloned.1.call-update) | async-done | bytes 65552 | tf_op jit(solution)/shard_map/psum | solution.py:58
  176.5 14.1 %all_gather.3 = f32[256,256]{1,0:T(8,128)S(1)} all-gather(f32[64,256]{1,0:T(8,128)} %all-reduce.3.cloned.1.call-done), channel_id=1, replica_groups=mesh['space'=8,'mode'=4] {'mode'}, dimensions={0}, use_global_device_ids=true | all-gather | bytes 327680 | tf_op jit(solution)/shard_map/all_gather | solution.py:59
  190.6 0.1 copy.35
  190.8 11.7 %cholesky.50 = f32[128,128]{1,0:T(8,128)S(1)} custom-call(f32[128,128]{1,0:T(8,128)S(1)} %cholesky.118), custom_call_target="Cholesky" | custom-call | tf_op jit(solution)/shard_map/jit(cholesky)/cholesky | solution.py:60
  202.6 9.8 %custom-call.15 = f32[1,128,128]{1,2,0:T(8,128)S(1)} custom-call(f32[1,128,128]{2,1,0:T(8,128)S(1)} %get-tuple-element.31), custom_call_target="InvertDiagBlocksLowerTriangular" | custom-call | tf_op jit(solution)/shard_map/jit(cholesky)/cholesky | solution.py:60
  212.4 0.2 constant_dynamic-update-slice_fusion.8
  212.6 0.3 convolution_subtract_fusion.1
  212.9 11.7 %cholesky.105 = f32[128,128]{1,0:T(8,128)S(1)} custom-call(f32[128,128]{1,0:T(8,128)S(1)} %convolution_subtract_fusion.1), custom_call_target="Cholesky" | custom-call | tf_op jit(solution)/shard_map/jit(cholesky)/cholesky | solution.py:60
  224.6 0.7 compare_reduce_fusion
  226.6 0.1 triangular_solve.63
  226.7 4.1 %while.1 = (s32[]{:T(128)}, f32[256,256]{1,0:T(8,128)S(1)}, s32[2,2]{1,0:T(2,128)S(1)}, f32[2,128,128]{2,1,0:T(8,128)S(1)}, s32[]{:T(128)}) while((s32[]{:T(128)}, f32[256,256]{1,0:T(8,128)S(1)}, s32[2,2]{1,0:T(2,128)S(1)}, f32[2,128,128]{2,1,0:T(8,128)S(1)}, s32[]{:T(128)}) %tuple.26), condition=%wide.while_cond, body=%wide.while_body.sunk | while | flops 2 | bytes 131181 | solution.py:62
  226.9 0.6 fusion.45
  227.5 1.4 bitcast_dynamic-update-slice_fusion.2
  228.9 0.6 fusion.45
  229.5 1.4 bitcast_dynamic-update-slice_fusion.2
  230.8 19.7 %custom-call.16 = f32[2,128,128]{1,2,0:T(8,128)S(1)} custom-call(f32[2,128,128]{2,1,0:T(8,128)S(1)} %get-tuple-element.13), custom_call_target="InvertDiagBlocksLowerTriangular" | custom-call | tf_op jit(solution)/shard_map/jit(_solve_triangular)/triangular_solve | solution.py:62
  250.5 0.3 fusion.18
  250.8 0.3 convolution_subtract_fusion
  251.0 0.3 fusion.23
  251.4 4.8 %fusion.6 = f32[64,3072]{1,0:T(8,128)} fusion(f32[512,3072]{1,0:T(8,128)} %copy-done, s32[]{:T(128)S(6)} %select_n.28, s32[]{:T(128)S(6)} %select_n.30, f32[128,256]{1,0:T(8,128)S(1)} %fusion.18, f32[128,256]{1,0:T(8,128)S(1)} %fusion.23), kind=kOutput, calls=%fused_computation.12 | convolution fusion | flops 603996160 | bytes 4194312 | tf_op jit(solution)/shard_map/dot_general | solution.py:64
  (25 shorter events, 0.3 us)
Async XLA Ops:
  6.5 169.9 %all-reduce.3.cloned.1.call-start = ((), (), s32[]{:S(2)}) async-start(), calls=%async_computation | async-start | bytes 131072 | tf_op jit(solution)/shard_map/psum | solution.py:58
  8.4 5.9 %collective-permute-start = (bf16[64,384]{1,0:T(8,128)(2,1)S(1)}, bf16[64,384]{1,0:T(8,128)(2,1)S(1)}, u32[]{:S(2)}, u32[]{:S(2)}) collective-permute-start(bf16[64,384]{1,0:T(8,128)(2,1)S(1)} %get-tuple-element.26), channel_id=1, source_target_pairs={{0,4},{4,8},{8,12},{12,16},{16,20},{20,24},{24,28},{28,0},{1,5},{5... | collective-permute-start | bytes 147464 | tf_op jit(solution)/shard_map/ppermute | solution.py:18
  9.0 5.4 %collective-permute-start.1 = (bf16[64,384]{1,0:T(8,128)(2,1)S(1)}, bf16[64,384]{1,0:T(8,128)(2,1)S(1)}, u32[]{:S(2)}, u32[]{:S(2)}) collective-permute-start(bf16[64,384]{1,0:T(8,128)(2,1)S(1)} %get-tuple-element.27), channel_id=1, source_target_pairs={{4,0},{8,4},{12,8},{16,12},{20,16},{24,20},{28,24},{0,28},{5,1},{9... | collective-permute-start | bytes 147464 | tf_op jit(solution)/shard_map/ppermute | solution.py:20
  18.1 13.3 %copy-start.1 = (f32[64,3072]{1,0:T(8,128)S(1)}, f32[64,3072]{1,0:T(8,128)}, u32[]{:S(2)}) copy-start(f32[64,3072]{1,0:T(8,128)} %param.7) | copy-start | bytes 2359300
  31.5 4.5 %collective-permute-start.2 = (bf16[64,384]{1,0:T(8,128)(2,1)S(1)}, bf16[64,384]{1,0:T(8,128)(2,1)S(1)}, u32[]{:S(2)}, u32[]{:S(2)}) collective-permute-start(bf16[64,384]{1,0:T(8,128)(2,1)S(1)} %get-tuple-element.24), channel_id=1, source_target_pairs={{0,4},{4,8},{8,12},{12,16},{16,20},{20,24},{24,28},{28,0},{1,5},{5... | collective-permute-start | bytes 147464 | tf_op jit(solution)/shard_map/ppermute | solution.py:18
  32.3 3.7 %collective-permute-start.3 = (bf16[64,384]{1,0:T(8,128)(2,1)S(1)}, bf16[64,384]{1,0:T(8,128)(2,1)S(1)}, u32[]{:S(2)}, u32[]{:S(2)}) collective-permute-start(bf16[64,384]{1,0:T(8,128)(2,1)S(1)} %get-tuple-element.25), channel_id=1, source_target_pairs={{4,0},{8,4},{12,8},{16,12},{20,16},{24,20},{28,24},{0,28},{5,1},{9... | collective-permute-start | bytes 147464 | tf_op jit(solution)/shard_map/ppermute | solution.py:20
  55.2 22.5 %collective-permute-start.4 = (f32[64,3072]{1,0:T(8,128)S(1)}, f32[64,3072]{1,0:T(8,128)S(1)}, u32[]{:S(2)}, u32[]{:S(2)}) collective-permute-start(f32[64,3072]{1,0:T(8,128)S(1)} %subtract_multiply_fusion), channel_id=1, source_target_pairs={{0,1},{1,2},{2,3},{3,0},{4,5},{5,6},{6,7},{7,4},{8,9},{9,10},{10,1... | collective-permute-start | bytes 2359304 | tf_op jit(solution)/shard_map/ppermute | solution.py:51
  77.6 21.1 %collective-permute-start.5 = (f32[64,3072]{1,0:T(8,128)S(1)}, f32[64,3072]{1,0:T(8,128)S(1)}, u32[]{:S(2)}, u32[]{:S(2)}) collective-permute-start(f32[64,3072]{1,0:T(8,128)S(1)} %collective-permute-done.4), channel_id=1, source_target_pairs={{0,1},{1,2},{2,3},{3,0},{4,5},{5,6},{6,7},{7,4},{8,9},{9,10},{10,1... | collective-permute-start | bytes 2359304 | tf_op jit(solution)/shard_map/ppermute | solution.py:51
  98.7 20.2 %collective-permute-start.6 = (f32[64,3072]{1,0:T(8,128)S(1)}, f32[64,3072]{1,0:T(8,128)S(1)}, u32[]{:S(2)}, u32[]{:S(2)}) collective-permute-start(f32[64,3072]{1,0:T(8,128)S(1)} %collective-permute-done.5), channel_id=1, source_target_pairs={{0,1},{1,2},{2,3},{3,0},{4,5},{5,6},{6,7},{7,4},{8,9},{9,10},{10,1... | collective-permute-start | bytes 2359304 | tf_op jit(solution)/shard_map/ppermute | solution.py:51
  119.4 2.6 %copy-start = (f32[512,3072]{1,0:T(8,128)}, f32[512,3072]{1,0:T(8,128)S(1)}, u32[]{:S(2)}) copy-start(f32[512,3072]{1,0:T(8,128)S(1)} %constant_dynamic-update-slice_fusion) | copy-start | bytes 18874372
Sparse Core Ops, SparseCore 0:
  125.8 50.5 all-reduce.2
